TPU v7x, 32 devices: a whole 2x2x4 slice. The times are simulated.
32 devices in a mesh: dp: 8 (over z, x), tensor: 4 (over y, core).
Axes of the slice: x: 2, y: 2, z: 4, core: 2. Of those that a mesh axis runs over, the one named last changes fastest.
Arguments:
- codons: int32 [32, 1024], P(('dp', 'tensor')), may hold values from 0 to 69
- segments: int32 [32, 1024], P('dp'), may hold values from 0 to 3, never falling along the last dimension, each value on 1 to 512 neighbouring positions
- targets: int32 [32, 1024], P(('dp', 'tensor')), may hold values from 0 to 69
- loss_mask: int32 [32, 1024], P(('dp', 'tensor')), may hold values 0 or 1
- owner_map: int32 [192], replicated, may hold values from 0 to 191, as said below
- step_count: int32 [], replicated, may hold values from 2 to 20
- block_weight: float32 [4, 192, 96, 96], P('tensor', 'dp')
- block_left: float32 [4, 192, 96, 96], P('tensor', 'dp'), as said below
- block_right: float32 [4, 192, 96, 96], P('tensor', 'dp'), as said below
- block_left_root: float32 [4, 192, 96, 96], P('tensor', 'dp'), as said below
- block_right_root: float32 [4, 192, 96, 96], P('tensor', 'dp'), as said below
- embedding_weight: float32 [128, 768], replicated, may hold values from -0.4375 to 0.4375
- table_left: float32 [128, 128], replicated, as said below
- table_right: float32 [768, 768], replicated, as said below
- table_left_root: float32 [128, 128], replicated, as said below
- table_right_root: float32 [768, 768], replicated, as said below
- norm_params: float32 [6, 768], replicated, as said below
- norm_moment: float32 [6, 768], replicated, may hold values from -1.1444092e-05 to 1.1444092e-05
- norm_second: float32 [6, 768], replicated, may hold values from 5.57041e-14 to 2.228164e-13
Outputs:
- loss_value: float32 [], replicated
- grad_norm: float32 [], replicated
- block_grad: float32 [4, 192, 96, 96], P('tensor', 'dp')
- new_block_left: float32 [4, 192, 96, 96], P('tensor', 'dp')
- new_block_right: float32 [4, 192, 96, 96], P('tensor', 'dp')
- new_block_weight: float32 [4, 192, 96, 96], P('tensor', 'dp')
- embedding_clipped_gradient: float32 [128, 768], replicated
- new_table_left: float32 [128, 128], replicated
- new_table_right: float32 [768, 768], replicated
- new_table_weight: float32 [128, 768], replicated
- norm_clipped_gradient: float32 [6, 768], replicated
- new_norm_moment: float32 [6, 768], replicated
- new_norm_second: float32 [6, 768], replicated
- new_norm_params: float32 [6, 768], replicated
Inputs may be any that keep to these rules, and one draw needn't show every extreme that they name: owner_map is a permutation. `block_left`: symmetric. `block_right`: symmetric. `block_left_root`: symmetric positive definite. `block_right_root`: symmetric positive definite. `table_left`: symmetric. `table_right`: symmetric. `table_left_root`: symmetric positive definite. `table_right_root`: symmetric positive definite. `norm_params`: rows 0, 2, 4 are gains, rows 1, 3, 5 biases.
All inputs are finite; a program needn't handle non-finite values. No bound on the sum of `loss_mask` on one device may be relied on, other than what follows from the above.
Results may differ from a plain program's by a relative error of at most 0.0013.
The roundings to bfloat16 on the way count: a program that leaves them out, or rounds other values in their place, can miss the bound.
Values may be sent and summed in bfloat16 or wider, within the bound.
A program may use at most 256 MiB of HBM per device.

v0:
```python
import math

import jax
import jax.numpy as jnp
from jax import lax
from jax.sharding import PartitionSpec as P

FF = 3072
HS = 64


CLIP_LEVEL = 0.005
STAT_DECAY = 0.5
MATRIX_RATE = 0.03
WEIGHT_DECAY = 0.01
VECTOR_RATE = 0.2
FIRST_BETA = 0.9
SECOND_BETA = 0.999
ADAM_EPSILON = 1e-08
NORM_EPSILON = 1e-05
ROOT_EPSILON = 1e-06
MASK_VALUE = -1e30
ROTARY_BASE = 10000.0
TOP_PRECISION = lax.Precision.HIGHEST


def layer_norm(values, gain_row, bias_row):
    center = values - jnp.mean(values, -1, keepdims=True)
    spread = jnp.mean(center * center, -1, keepdims=True)
    return center * lax.rsqrt(spread + NORM_EPSILON) * gain_row + bias_row


def exact_gelu(values):
    return jax.nn.gelu(values, approximate=False)


def rotary_tables(length, width):
    half_width = width // 2
    freqs = jnp.exp(
        -math.log(ROTARY_BASE) * (2.0 * jnp.arange(half_width, dtype=jnp.float32) / width)
    )
    angles = jnp.arange(length, dtype=jnp.float32)[:, None] * freqs[None, :]
    return (jnp.cos(angles), jnp.sin(angles))


def rotate(values, cosine, sine):
    half_width = values.shape[-1] // 2
    front = values[..., :half_width]
    behind = values[..., half_width:]
    cos_col = cosine[:, None, :]
    sin_col = sine[:, None, :]
    return jnp.concatenate(
        [front * cos_col - behind * sin_col, behind * cos_col + front * sin_col], -1
    )


def tile_blocks(blocks, block_rows, block_columns):
    leading = blocks.shape[0]
    block_edge = blocks.shape[-1]
    shaped = blocks.reshape(leading, block_rows, block_columns, block_edge, block_edge)
    return shaped.transpose(0, 1, 3, 2, 4).reshape(
        leading, block_rows * block_edge, block_columns * block_edge
    )


def untile(matrix, block_edge):
    leading = matrix.shape[0]
    height = matrix.shape[1] // block_edge
    across = matrix.shape[2] // block_edge
    shaped = matrix.reshape(leading, height, block_edge, across, block_edge)
    return shaped.transpose(0, 1, 3, 2, 4).reshape(leading, height * across, block_edge, block_edge)


def block_layout(width, shard_width, shard_ff, block_edge):
    model_blocks = width // block_edge
    return [
        (model_blocks, 3 * shard_width // block_edge),
        (shard_width // block_edge, model_blocks),
        (model_blocks, shard_ff // block_edge),
        (shard_ff // block_edge, model_blocks),
    ]


def spread_rows(values):
    return lax.all_gather(values, "tensor", axis=0, tiled=True)


def merge_rows(values):
    return lax.psum_scatter(values, "tensor", scatter_dimension=0, tiled=True)


def spread_grads(values):
    return lax.all_gather(values, "tensor", axis=0, tiled=True)


def merge_grads(values):
    return lax.psum_scatter(values, "tensor", scatter_dimension=0, tiled=True)


def masked_scores(chosen, keys, segment, offset, block_rows):
    same = segment[offset : offset + block_rows, None] == segment[None, :]
    scores = jnp.einsum("qhd,khd->hqk", chosen, keys, preferred_element_type=jnp.float32)
    return jnp.where(same[None], scores, MASK_VALUE)


def attend_forward(query, keys, values, segment):
    length = query.shape[0]
    block_rows = min(512, length)
    outputs = []
    totals = []
    for offset in range(0, length, block_rows):
        scores = masked_scores(
            query[offset : offset + block_rows], keys, segment, offset, block_rows
        )
        top_score = jnp.max(scores, -1, keepdims=True)
        weights = jnp.exp(scores - top_score)
        summed = jnp.sum(weights, -1, keepdims=True)
        probs = weights / summed
        outputs.append(
            jnp.einsum(
                "hqk,khd->qhd",
                probs.astype(jnp.bfloat16),
                values,
                preferred_element_type=jnp.float32,
            )
        )
        totals.append((top_score + jnp.log(summed))[..., 0])
    return (jnp.concatenate(outputs, 0), jnp.concatenate(totals, 1))


def attend_backward(query, keys, values, segment, grad_out, log_total):
    length = query.shape[0]
    block_rows = min(512, length)
    query_parts = []
    key_grad = jnp.zeros(keys.shape, jnp.float32)
    value_grad = jnp.zeros(values.shape, jnp.float32)
    for offset in range(0, length, block_rows):
        chosen = query[offset : offset + block_rows]
        grad_block = grad_out[offset : offset + block_rows]
        scores = masked_scores(chosen, keys, segment, offset, block_rows)
        probs = jnp.exp(scores - log_total[:, offset : offset + block_rows, None])
        grad_probs = jnp.einsum(
            "qhd,khd->hqk", grad_block, values, preferred_element_type=jnp.float32
        )
        delta = jnp.sum(probs * grad_probs, -1, keepdims=True)
        grad_scores = (probs * (grad_probs - delta)).astype(jnp.bfloat16)
        query_parts.append(
            jnp.einsum("hqk,khd->qhd", grad_scores, keys, preferred_element_type=jnp.float32)
        )
        key_grad = key_grad + jnp.einsum(
            "hqk,qhd->khd", grad_scores, chosen, preferred_element_type=jnp.float32
        )
        value_grad = value_grad + jnp.einsum(
            "hqk,qhd->khd",
            probs.astype(jnp.bfloat16),
            grad_block,
            preferred_element_type=jnp.float32,
        )
    return (jnp.concatenate(query_parts, 0), key_grad, value_grad)


def shampoo(grad, left, right, left_root, right_root, weight):
    new_left = STAT_DECAY * left + (1.0 - STAT_DECAY) * jnp.einsum(
        "...ij,...kj->...ik", grad, grad, precision=TOP_PRECISION
    )
    new_right = STAT_DECAY * right + (1.0 - STAT_DECAY) * jnp.einsum(
        "...ji,...jk->...ik", grad, grad, precision=TOP_PRECISION
    )
    partial_left = jnp.einsum("...ij,...jk->...ik", left_root, grad, precision=TOP_PRECISION)
    precond = jnp.einsum("...ij,...jk->...ik", partial_left, right_root, precision=TOP_PRECISION)
    scale_back = lax.rsqrt(jnp.mean(precond * precond, axis=(-2, -1), keepdims=True) + ROOT_EPSILON)
    new_weight = weight * (1.0 - MATRIX_RATE * WEIGHT_DECAY) - MATRIX_RATE * precond * scale_back
    return (new_left, new_right, new_weight)


def adamw(grad, moment, second, weight, step_value):
    new_moment = FIRST_BETA * moment + (1.0 - FIRST_BETA) * grad
    new_second = SECOND_BETA * second + (1.0 - SECOND_BETA) * grad * grad
    corrected_one = new_moment / (1.0 - FIRST_BETA**step_value)
    corrected_two = new_second / (1.0 - SECOND_BETA**step_value)
    new_weight = weight - VECTOR_RATE * (
        corrected_one / (jnp.sqrt(corrected_two) + ADAM_EPSILON) + WEIGHT_DECAY * weight
    )
    return (new_moment, new_second, new_weight)


def body(
    codons,
    segments,
    targets,
    loss_mask,
    owner_map,
    step_count,
    block_weight,
    block_left,
    block_right,
    block_left_root,
    block_right_root,
    embedding_weight,
    table_left,
    table_right,
    table_left_root,
    table_right_root,
    norm_params,
    norm_moment,
    norm_second,
):
    width = embedding_weight.shape[1]
    vocab_size = embedding_weight.shape[0]
    shards = lax.axis_size("tensor")
    shard_width = width // shards
    shard_ff = FF // shards
    block_edge = block_weight.shape[-1]
    slot_count = block_weight.shape[1]
    heads_shard = shard_width // HS
    bf16 = jnp.bfloat16
    single_float = jnp.float32
    gathered = lax.all_gather(block_weight[0].astype(bf16), "dp", axis=0, tiled=True)[None]
    movers = (spread_rows, merge_rows, spread_grads, merge_grads)
    spread_in, merge_out, spread_back, merge_back = movers
    shard_count = gathered.shape[0]
    head_total = shard_count * heads_shard
    ordered = gathered[:, owner_map]
    matrices = []
    offset = 0
    for block_rows, block_columns in block_layout(width, shard_width, shard_ff, block_edge):
        matrices.append(
            tile_blocks(
                ordered[:, offset : offset + block_rows * block_columns], block_rows, block_columns
            )
        )
        offset = offset + block_rows * block_columns
    projection_weight, output_matrix, expansion_weight, contract_weight = matrices
    vocab_index = jnp.arange(vocab_size, dtype=jnp.int32)
    codon_onehot_rows = (codons[..., None] == vocab_index).astype(single_float)
    embed_scale = math.sqrt(width)
    embedded = embed_scale * jnp.einsum(
        "ncg,gt->nct", codon_onehot_rows, embedding_weight, precision=TOP_PRECISION
    )
    normed = layer_norm(embedded, norm_params[0], norm_params[1]).astype(bf16)
    normalized_full_rows = spread_in(normed)
    group = normalized_full_rows.shape[0]
    length = normalized_full_rows.shape[1]
    projection_output = jnp.einsum(
        "bma,fac->bmfc",
        normalized_full_rows,
        projection_weight,
        preferred_element_type=single_float,
    )
    cosine, sine = rotary_tables(length, HS)

    def heads_of(component):
        return projection_output[
            ..., component * shard_width : (component + 1) * shard_width
        ].reshape(group, length, head_total, HS)

    query = (rotate(heads_of(0), cosine, sine) * HS ** (-0.5)).astype(bf16)
    keys = rotate(heads_of(1), cosine, sine).astype(bf16)
    values = heads_of(2).astype(bf16)
    attention_output, log_total = lax.map(
        lambda packed: attend_forward(*packed), (query, keys, values, segments)
    )
    attention_output = attention_output.astype(bf16).reshape(
        group, length, shard_count, shard_width
    )
    branch = merge_out(
        jnp.einsum(
            "mgjq,jqr->mgr", attention_output, output_matrix, preferred_element_type=single_float
        )
    )
    middle = embedded + branch
    normed_two = layer_norm(middle, norm_params[2], norm_params[3]).astype(bf16)
    second_normalized_full = spread_in(normed_two)
    hidden_state = jnp.einsum(
        "iyr,krv->iykv",
        second_normalized_full,
        expansion_weight,
        preferred_element_type=single_float,
    )
    active_units = exact_gelu(hidden_state).astype(bf16)
    branch_two = merge_out(
        jnp.einsum(
            "rxum,ume->rxe", active_units, contract_weight, preferred_element_type=single_float
        )
    )
    final_in = middle + branch_two
    final = layer_norm(final_in, norm_params[4], norm_params[5])
    final_reduced_precision = final.astype(bf16)
    embedding_reduced_precision = embedding_weight.astype(bf16)
    output_scores = jnp.einsum(
        "hxt,qt->hxq",
        final_reduced_precision,
        embedding_reduced_precision,
        preferred_element_type=single_float,
    )
    shifted = output_scores - jnp.max(output_scores, -1, keepdims=True)
    log_probs = shifted - jnp.log(jnp.sum(jnp.exp(shifted), -1, keepdims=True))
    target_hot = (targets[..., None] == vocab_index).astype(single_float)
    mask_values = loss_mask.astype(single_float)
    picked = jnp.sum(target_hot * log_probs, -1)
    loss_sum, mask_total = lax.psum(
        (-jnp.sum(mask_values * picked), jnp.sum(mask_values)), ("dp", "tensor")
    )
    token_count = jnp.maximum(mask_total, 1.0)
    loss_value = loss_sum / token_count
    logit_gradient = (
        (jnp.exp(log_probs) - target_hot) * (mask_values / token_count)[..., None]
    ).astype(bf16)
    embedding_clipped_gradient = jnp.einsum(
        "gux,gup->xp", logit_gradient, final_reduced_precision, preferred_element_type=single_float
    )
    final_gradient = jnp.einsum(
        "ncg,gt->nct",
        logit_gradient,
        embedding_reduced_precision,
        preferred_element_type=single_float,
    )
    _, final_back = jax.vjp(layer_norm, final_in, norm_params[4], norm_params[5])
    grad_final_in, gain_five, bias_five = final_back(final_gradient)
    second_branch_gradient = spread_back(grad_final_in.astype(bf16))
    contract_gradient = jnp.einsum(
        "hkey,hka->eya", active_units, second_branch_gradient, preferred_element_type=single_float
    )
    grad_active = jnp.einsum(
        "azc,mrc->azmr",
        second_branch_gradient,
        contract_weight,
        preferred_element_type=single_float,
    )
    _, gelu_back = jax.vjp(exact_gelu, hidden_state)
    hidden_gradient = gelu_back(grad_active)[0].astype(bf16)
    expand_grad = jnp.einsum(
        "crz,crix->izx",
        second_normalized_full,
        hidden_gradient,
        preferred_element_type=single_float,
    )
    grad_normed_two = merge_back(
        jnp.einsum(
            "brnm,njm->brj", hidden_gradient, expansion_weight, preferred_element_type=single_float
        )
    )
    _, second_back = jax.vjp(layer_norm, middle, norm_params[2], norm_params[3])
    grad_middle_norm, gain_three, bias_three = second_back(grad_normed_two)
    grad_middle = grad_final_in + grad_middle_norm
    branch_gradient = spread_back(grad_middle.astype(bf16))
    output_weight_gradient = jnp.einsum(
        "acpk,acx->pkx", attention_output, branch_gradient, preferred_element_type=single_float
    )
    grad_attended = jnp.einsum(
        "kgc,yvc->kgyv", branch_gradient, output_matrix, preferred_element_type=single_float
    )
    grad_attended = grad_attended.astype(bf16).reshape(group, length, head_total, HS)
    grad_query, grad_keys, grad_values = lax.map(
        lambda packed: attend_backward(*packed),
        (query, keys, values, segments, grad_attended, log_total),
    )
    grad_query_raw = rotate(grad_query * HS ** (-0.5), cosine, -sine)
    grad_keys_raw = rotate(grad_keys, cosine, -sine)
    projection_gradient = jnp.concatenate(
        [
            grad_query_raw.reshape(group, length, shard_count, shard_width),
            grad_keys_raw.reshape(group, length, shard_count, shard_width),
            grad_values.reshape(group, length, shard_count, shard_width),
        ],
        -1,
    ).astype(bf16)
    project_grad = jnp.einsum(
        "xnh,xnaf->ahf",
        normalized_full_rows,
        projection_gradient,
        preferred_element_type=single_float,
    )
    grad_normed = merge_back(
        jnp.einsum(
            "wbiv,iuv->wbu",
            projection_gradient,
            projection_weight,
            preferred_element_type=single_float,
        )
    )
    _, first_back = jax.vjp(layer_norm, embedded, norm_params[0], norm_params[1])
    grad_embed_norm, gain_one, bias_one = first_back(grad_normed)
    embedded_gradient = grad_middle + grad_embed_norm
    embedding_clipped_gradient = embedding_clipped_gradient + embed_scale * jnp.einsum(
        "gux,gup->xp", codon_onehot_rows, embedded_gradient, precision=TOP_PRECISION
    )
    norm_grad = jnp.stack([gain_one, bias_one, gain_three, bias_three, gain_five, bias_five])
    embedding_clipped_gradient, norm_grad = lax.psum(
        (embedding_clipped_gradient, norm_grad), ("dp", "tensor")
    )
    block_grads = jnp.concatenate(
        [
            untile(project_grad, block_edge),
            untile(output_weight_gradient, block_edge),
            untile(expand_grad, block_edge),
            untile(contract_gradient, block_edge),
        ],
        1,
    )
    block_total = owner_map.shape[0]
    slot_order = (
        jnp.zeros((block_total,), jnp.int32)
        .at[owner_map]
        .set(jnp.arange(block_total, dtype=jnp.int32))
    )
    slot_grads = block_grads[:, slot_order]
    slot_grads = slot_grads[0]
    summed_all = lax.psum(slot_grads, "dp")
    owned = lax.dynamic_slice_in_dim(summed_all, lax.axis_index("dp") * slot_count, slot_count, 0)
    square_sum = lax.psum(jnp.sum(owned * owned), ("dp", "tensor"))
    square_sum = (
        square_sum
        + jnp.sum(embedding_clipped_gradient * embedding_clipped_gradient)
        + jnp.sum(norm_grad * norm_grad)
    )
    grad_norm = jnp.sqrt(square_sum)
    factor = CLIP_LEVEL / jnp.maximum(grad_norm, CLIP_LEVEL)
    block_grad = owned * factor
    new_left, new_right, new_weight = shampoo(
        block_grad,
        block_left[0],
        block_right[0],
        block_left_root[0],
        block_right_root[0],
        block_weight[0],
    )
    table_clipped = embedding_clipped_gradient * factor
    table_left_new, table_right_new, table_weight_new = shampoo(
        table_clipped, table_left, table_right, table_left_root, table_right_root, embedding_weight
    )
    norm_clipped = norm_grad * factor
    moment_new, second_new, params_new = adamw(
        norm_clipped, norm_moment, norm_second, norm_params, step_count.astype(single_float)
    )
    return (
        loss_value,
        grad_norm,
        block_grad[None],
        new_left[None],
        new_right[None],
        new_weight[None],
        table_clipped,
        table_left_new,
        table_right_new,
        table_weight_new,
        norm_clipped,
        moment_new,
        second_new,
        params_new,
    )


def solution(mesh):
    in_specs = (
        P(("dp", "tensor"), None),
        P("dp", None),
        P(("dp", "tensor"), None),
        P(("dp", "tensor"), None),
        P(),
        P(),
        P("tensor", "dp", None, None),
        P("tensor", "dp", None, None),
        P("tensor", "dp", None, None),
        P("tensor", "dp", None, None),
        P("tensor", "dp", None, None),
        P(),
        P(),
        P(),
        P(),
        P(),
        P(),
        P(),
        P(),
    )
    out_specs = (
        P(),
        P(),
        P("tensor", "dp", None, None),
        P("tensor", "dp", None, None),
        P("tensor", "dp", None, None),
        P("tensor", "dp", None, None),
        P(),
        P(),
        P(),
        P(),
        P(),
        P(),
        P(),
        P(),
    )
    return jax.shard_map(body, mesh=mesh, in_specs=in_specs, out_specs=out_specs, check_vma=False)
```

profile of v0, /device:TPU:0, one launch (start us, length us, event | category | flops | bytes accessed | tf_op | source)
XLA Modules:
  0.0 1627.6 jit_solution(16524558720702222583)
XLA Ops:
  19.6 73.8 %all-gather.16.cloned.1.call-done = bf16[1,192,96,96]{3,2,0,1:T(8,128)(2,1)} async-done(((bf16[1,24,96,96]{3,2,0,1:T(8,128)(2,1)}), bf16[1,192,96,96]{3,2,0,1:T(8,128)(2,1)}) %all-gather.16.cloned.1.call-update) | async-done | bytes 3538960 | tf_op jit(solution)/shard_map/all_gather | solution.py:218
  93.4 5.7 gather_fusion
  108.4 31.7 %all-gather.14.cloned.1.call-done = bf16[4096,768]{0,1:T(8,128)(2,1)} async-done(((bf16[1024,768]{0,1:T(8,128)(2,1)}), bf16[4096,768]{0,1:T(8,128)(2,1)}) %all-gather.14.cloned.1.call-update) | async-done | bytes 6291472 | tf_op jit(solution)/shard_map/all_gather | solution.py:85
  140.1 8.7 copy.166
  148.8 6.2 convolution_bitcast_fusion.2
  164.0 58.2 %while.28 = (s32[]{:T(128)}, bf16[4,1024,3,64]{1,3,2,0:T(8,128)(2,1)}, f32[4,3,1024]{2,1,0:T(4,128)}, bf16[4,1024,3,64]{1,3,2,0:T(8,128)(2,1)}, s32[4,1024]{1,0:...) while((s32[]{:T(128)}, bf16[4,1024,3,64]{1,3,2,0:T(8,128)(2,1)}, ...), condition=%wide.region_7.8_spmd.clone, body=%wide.region_2.7_spmd.sunk.clone | while | flops 835452928 | bytes 51542680 | solution.py:260
  169.6 3.3 fusion.274
  222.1 8.2 fusion.188
  230.4 99.2 %reduce-scatter.5.cloned.1.call-done = f32[1,1024,768]{1,2,0:T(8,128)} async-done(((f32[4,1024,768]{1,2,0:T(8,128)}), f32[1,1024,768]{1,2,0:T(8,128)}) %reduce-scatter.5.cloned.1.call-update) | async-done | bytes 3145744 | tf_op jit(solution)/shard_map/reduce_scatter | solution.py:89
  329.6 4.0 fusion.181
  347.8 3.3 copy.120
  351.1 3.8 reshape.869
  354.9 31.1 %all-gather.8.cloned.1.call-done = bf16[4,1024,768]{2,1,0:T(8,128)(2,1)} async-done(((bf16[1,1024,768]{2,1,0:T(8,128)(2,1)}), bf16[4,1024,768]{2,1,0:T(8,128)(2,1)}) %all-gather.8.cloned.1.call-update) | async-done | bytes 6291472 | tf_op jit(solution)/shard_map/all_gather | solution.py:85
  386.0 10.7 fusion.119
  396.7 4.5 copy-done.3
  401.2 28.1 %fusion.77 = f32[4,1024,768]{1,2,0:T(8,128)} fusion(f32[4,1024,768]{1,2,0:T(8,128)S(1)} %get-tuple-element.224, u8[1024,768]{0,1:T(8,128)(4,1)S(1)} %get-tuple-element.112, u8[1024,768]{0,1:T(8,128)(4,1)S(1)} %get-tuple-element.111), kind=kLoop, calls=%fused_computation.109 | loop fusion | flops 210763776 | bytes 26738688 | tf_op jit(solution)/shard_map/erfc | solution.py:34
  429.3 21.6 %fusion.100 = f32[4,1024,768]{1,2,0:T(8,128)} fusion(bf16[768,768,1]{1,0,2:T(8,128)(2,1)S(1)} %reshape.870, f32[4,1024,768]{1,2,0:T(8,128)} %fusion.77, f32[4,1024,768]{1,2,0:T(8,128)} %copy-done.3), kind=kOutput, calls=%fused_computation.151 | convolution fusion | flops 4841275392 | bytes 38928384 | tf_op jit(solution)/shard_map/rxum,ume->rxe/dot_general | solution.py:282
  451.0 99.2 %reduce-scatter.7.cloned.1.call-done = f32[1,1024,768]{1,2,0:T(8,128)} async-done(((f32[4,1024,768]{1,2,0:T(8,128)}), f32[1,1024,768]{1,2,0:T(8,128)}) %reduce-scatter.7.cloned.1.call-update) | async-done | bytes 3145744 | tf_op jit(solution)/shard_map/reduce_scatter | solution.py:89
  550.2 3.9 fusion.180
  558.0 39.5 %psum.43 = f32[]{:T(128)} all-reduce(f32[]{:T(128)} %get-tuple-element.128), channel_id=1, replica_groups=mesh['dp'=8,'tensor'=4] {'dp','tensor'}, use_global_device_ids=true, to_apply=%region_20.21 | all-reduce | flops 1 | bytes 8 | tf_op jit(solution)/shard_map/psum | solution.py:301
  601.1 3.5 copy.124
  604.6 4.5 fusion.110
  616.2 4.0 reshape.817
  620.1 43.4 %all-gather.10.cloned.1.call-done = bf16[4,1024,768]{2,1,0:T(8,128)(2,1)} async-done(((bf16[1,1024,768]{2,1,0:T(8,128)(2,1)}), bf16[4,1024,768]{2,1,0:T(8,128)(2,1)}) %all-gather.10.cloned.1.call-update) | async-done | bytes 6291472 | tf_op jit(solution)/shard_map/all_gather | solution.py:93
  663.6 16.7 %add_convert_fusion = bf16[4,1024,768]{1,2,0:T(8,128)(2,1)} fusion(f32[4,1024,768]{1,2,0:T(8,128)} %fusion.77, f32[4,1024,768]{1,2,0:T(8,128)} %copy-done.3, bf16[4,1024,768]{2,1,0:T(8,128)(2,1)} %all-gather.10.cloned.1.call-done, bf16[768,768,1]{1,0,2:T(8,128)(2,1)S(1)} %copy-done.35), kind=kOutput, calls=%fused_computation.135 | convolution fusion | flops 4875878400 | bytes 38928384 | tf_op jit(solution)/shard_map/azc,mrc->azmr/dot_general | solution.py:324
  680.3 14.2 fusion.141
  694.6 99.2 %reduce-scatter.9.cloned.1.call-done = f32[1,1024,768]{1,2,0:T(8,128)} async-done(((f32[4,1024,768]{1,2,0:T(8,128)}), f32[1,1024,768]{1,2,0:T(8,128)}) %reduce-scatter.9.cloned.1.call-update) | async-done | bytes 3145744 | tf_op jit(solution)/shard_map/reduce_scatter | solution.py:97
  793.8 4.6 multiply_reduce_fusion.2
  805.7 46.5 %all-gather.12.cloned.1.call-done = bf16[4,1024,768]{2,1,0:T(8,128)(2,1)} async-done(((bf16[1,1024,768]{2,1,0:T(8,128)(2,1)}), bf16[4,1024,768]{2,1,0:T(8,128)(2,1)}) %all-gather.12.cloned.1.call-update) | async-done | bytes 6291472 | tf_op jit(solution)/shard_map/all_gather | solution.py:93
  852.2 6.1 convolution_convert_fusion
  858.3 166.7 %while.29 = (s32[]{:T(128)}, f32[4,1024,3,64]{1,3,2,0:T(8,128)}, f32[4,1024,3,64]{1,3,2,0:T(8,128)}, bf16[4,1024,3,64]{1,3,2,0:T(8,128)(2,1)}, bf16[4,1024,3,64]...) while((s32[]{:T(128)}, f32[4,1024,3,64]{1,3,2,0:T(8,128)}, ...), condition=%wide.region_29.30_spmd.clone, body=%wide.region_26.29_spmd.sunk.clone | while | flops 2052649984 | bytes 160057152 | solution.py:354
  862.4 5.9 multiply_reduce_fusion.18
  870.3 5.8 multiply_reduce_fusion.19
  876.1 7.9 multiply_convert_fusion.9
  904.0 5.9 multiply_reduce_fusion.18
  911.9 5.8 multiply_reduce_fusion.19
  917.7 7.9 multiply_convert_fusion.9
  945.5 5.9 multiply_reduce_fusion.18
  953.4 5.8 multiply_reduce_fusion.19
  959.2 7.9 multiply_convert_fusion.9
  987.1 5.9 multiply_reduce_fusion.18
  994.9 5.8 multiply_reduce_fusion.19
  1000.7 7.9 multiply_convert_fusion.9
  1031.7 8.9 fusion.120
  1042.1 29.4 %fusion.80 = bf16[768,4,1024]{2,0,1:T(8,128)(2,1)} fusion(f32[4,1024,768]{1,2,0:T(8,128)} %copy-done.3), kind=kLoop, calls=%fused_computation.112 | loop fusion | flops 204472320 | bytes 18874368 | tf_op jit(solution)/shard_map/convert_element_type | solution.py:280
  1071.4 11.6 convolution_bitcast_fusion.3
  1083.0 4.4 reshape.826
  1087.4 3.6 copy.137
  1091.0 8.8 copy.138
  1099.8 11.9 fusion.101
  1111.8 7.9 fusion.125
  1119.6 3.7 reshape.822
  1126.4 8.5 copy.134
  1134.9 5.1 fusion.104
  1140.9 4.4 maximum_bitcast_fusion.3
  1145.3 8.4 gather_fusion.1
  1157.6 5.4 fusion.176
  1166.3 4.9 fusion.133
  1174.7 277.7 %all-reduce.4.cloned.1.call-done = f32[192,96,96]{2,1,0:T(8,128)} async-done(((f32[192,96,96]{2,1,0:T(8,128)}), f32[192,96,96]{2,1,0:T(8,128)}) %all-reduce.4.cloned.1.call-update) | async-done | bytes 7077904 | tf_op jit(solution)/shard_map/psum | solution.py:409
  1458.4 40.1 %all-reduce = (f32[]{:T(128)}, f32[]{:T(128)}, f32[6,768]{1,0:T(8,128)}) all-reduce(f32[]{:T(128)S(6)} %neg.39, f32[]{:T(128)} %multiply_reduce_fusion.9, f32[6,768]{1,0:T(8,128)} %stack.27), channel_id=1, replica_groups=mesh['dp'=8,'tensor'=4] {'dp','tensor'}, use_global_device_ids=true, to_apply=%region_18.19 | all-reduce | flops 4610 | bytes 36880 | tf_op jit(solution)/shard_map/psum | solution.py:301
  1500.5 84.2 %all-reduce.6.cloned.1.call-done = f32[128,768]{1,0:T(8,128)} async-done(((f32[128,768]{1,0:T(8,128)}), f32[128,768]{1,0:T(8,128)}) %all-reduce.6.cloned.1.call-update) | async-done | bytes 393232 | tf_op jit(solution)/shard_map/psum | solution.py:389
  1594.8 3.6 add_multiply_fusion
  1608.7 5.1 fusion.128
  1613.9 4.7 fusion.129
  (456 shorter events, 253.6 us)
Async XLA Ops:
  7.2 1592.1 %copy-start = (f32[768,768]{1,0:T(8,128)S(1)}, f32[768,768]{1,0:T(8,128)}, u32[]{:S(2)}) copy-start(f32[768,768]{1,0:T(8,128)} %param.38) | copy-start | bytes 7077892
  7.2 86.2 %all-gather.16.cloned.1.call-start = ((), (), s32[]{:S(2)}) async-start(), calls=%async_computation.14 | async-start | bytes 5308416 | tf_op jit(solution)/shard_map/all_gather | solution.py:218
  9.6 130.6 %all-gather.14.cloned.1.call-start = ((), (), s32[]{:S(2)}) async-start(), calls=%async_computation.13 | async-start | bytes 7864320 | tf_op jit(solution)/shard_map/all_gather | solution.py:85
  11.2 4.0 copy-start.75
  17.7 311.9 %reduce-scatter.5.cloned.1.call-start = ((), (), s32[]{:S(2)}) async-start(), calls=%async_computation.4 | async-start | bytes 15728640 | tf_op jit(solution)/shard_map/reduce_scatter | solution.py:89
  108.4 113.7 %copy-start.51 = (bf16[192,768,1]{1,0,2:T(8,128)(2,1)}, bf16[192,768,1]{1,0,2:T(8,128)(2,1)S(1)}, u32[]{:S(2)}) copy-start(bf16[192,768,1]{1,0,2:T(8,128)(2,1)S(1)} %reshape.868) | copy-start | bytes 884740
  230.3 155.7 %all-gather.8.cloned.1.call-start = ((), (), s32[]{:S(2)}) async-start(), calls=%async_computation.5 | async-start | bytes 7864320 | tf_op jit(solution)/shard_map/all_gather | solution.py:85
  339.5 210.7 %reduce-scatter.7.cloned.1.call-start = ((), (), s32[]{:S(2)}) async-start(), calls=%async_computation.6 | async-start | bytes 15728640 | tf_op jit(solution)/shard_map/reduce_scatter | solution.py:89
  347.8 81.5 %copy-start.34 = (bf16[768,768,1]{1,0,2:T(8,128)(2,1)}, bf16[768,768,1]{1,0,2:T(8,128)(2,1)S(1)}, u32[]{:S(2)}) copy-start(bf16[768,768,1]{1,0,2:T(8,128)(2,1)S(1)} %reshape.870) | copy-start | bytes 3538948
  396.7 4.5 copy-start.3
  451.0 212.6 %all-gather.10.cloned.1.call-start = ((), (), s32[]{:S(2)}) async-start(), calls=%async_computation.7 | async-start | bytes 7864320 | tf_op jit(solution)/shard_map/all_gather | solution.py:93
  557.1 47.5 %copy-start.19 = (f32[1024,128]{0,1:T(8,128)}, f32[1024,128]{0,1:T(8,128)S(1)}, u32[]{:S(2)}) copy-start(f32[1024,128]{0,1:T(8,128)S(1)} %get-tuple-element.226) | copy-start | bytes 1572868
  557.1 47.5 %copy-start.57 = (f32[1024]{0:T(1024)}, f32[1024]{0:T(1024)S(1)}, u32[]{:S(2)}) copy-start(f32[1024]{0:T(1024)S(1)} %get-tuple-element.225) | copy-start | bytes 12292
  557.2 47.4 %copy-start.67 = (f32[1024]{0:T(1024)}, f32[1024]{0:T(1024)S(1)}, u32[]{:S(2)}) copy-start(f32[1024]{0:T(1024)S(1)} %log.20) | copy-start | bytes 12292
  598.2 6.4 copy-start.80
  604.6 4.5 copy-start.10
  604.6 4.7 copy-start.14
  613.4 50.2 %copy-start.35 = (bf16[768,768,1]{1,0,2:T(8,128)(2,1)S(1)}, bf16[768,768,1]{1,0,2:T(8,128)(2,1)}, u32[]{:S(2)}) copy-start(bf16[768,768,1]{1,0,2:T(8,128)(2,1)} %copy-done.34) | copy-start | bytes 3538948
  616.1 177.6 %reduce-scatter.9.cloned.1.call-start = ((), (), s32[]{:S(2)}) async-start(), calls=%async_computation.8 | async-start | bytes 15728640 | tf_op jit(solution)/shard_map/reduce_scatter | solution.py:97
  663.6 16.7 %copy-start.50 = (bf16[768,768]{0,1:T(8,128)(2,1)S(1)}, bf16[768,768]{0,1:T(8,128)(2,1)}, u32[]{:S(2)}) copy-start(bf16[768,768]{0,1:T(8,128)(2,1)} %reshape.817) | copy-start | bytes 3538948
  694.5 99.3 %copy-start.60 = (f32[1024]{0:T(1024)S(1)}, f32[1024]{0:T(1024)}, u32[]{:S(2)}) copy-start(f32[1024]{0:T(1024)} %copy-done.59) | copy-start | bytes 12292
  694.5 99.3 %copy-start.70 = (f32[1024]{0:T(1024)S(1)}, f32[1024]{0:T(1024)}, u32[]{:S(2)}) copy-start(f32[1024]{0:T(1024)} %copy-done.69) | copy-start | bytes 12292
  694.5 99.3 %copy-start.72 = (f32[768]{0:T(1024)S(1)}, f32[768]{0:T(1024)}, u32[]{:S(2)}) copy-start(f32[768]{0:T(1024)} %get-tuple-element.124) | copy-start | bytes 9220
  694.5 103.9 %copy-start.85 = (f32[1024]{0:T(1024)S(1)}, f32[1024]{0:T(1024)}, u32[]{:S(2)}) copy-start(f32[1024]{0:T(1024)} %copy-done.84) | copy-start | bytes 12292
  694.5 157.6 %all-gather.12.cloned.1.call-start = ((), (), s32[]{:S(2)}) async-start(), calls=%async_computation.9 | async-start | bytes 7864320 | tf_op jit(solution)/shard_map/all_gather | solution.py:93
  793.7 4.7 copy-start.8
  793.8 4.7 copy-start.25
  803.0 49.2 %copy-start.52 = (bf16[192,768,1]{1,0,2:T(8,128)(2,1)S(1)}, bf16[192,768,1]{1,0,2:T(8,128)(2,1)}, u32[]{:S(2)}) copy-start(bf16[192,768,1]{1,0,2:T(8,128)(2,1)} %copy-done.51) | copy-start | bytes 884740
  805.6 352.0 %reduce-scatter.11.cloned.1.call-start = ((), (), s32[]{:S(2)}) async-start(), calls=%async_computation.11 | async-start | bytes 15728640 | tf_op jit(solution)/shard_map/reduce_scatter | solution.py:97
  858.7 3.7 copy-start.16
  862.4 5.9 copy-start.4
  900.3 3.7 copy-start.16
  904.0 5.9 copy-start.4
  941.8 3.7 copy-start.16
  945.5 5.9 copy-start.4
  983.3 3.7 copy-start.16
  987.0 5.9 copy-start.4
  1040.6 411.7 %all-reduce.4.cloned.1.call-start = ((), (), s32[]{:S(2)}) async-start(), calls=%async_computation.10 | async-start | bytes 18874368 | tf_op jit(solution)/shard_map/psum | solution.py:409
  1099.8 11.9 copy-start.33
  1099.8 11.9 copy-start.40
  1099.8 11.9 copy-start.42
  1134.9 5.1 copy-start.21
  1134.9 5.1 copy-start.26
  1134.9 6.0 copy-start.36
  1153.7 3.9 copy-start.62
  1153.7 3.9 copy-start.76
  1153.8 430.9 %all-reduce.6.cloned.1.call-start = ((), (), s32[]{:S(2)}) async-start(), calls=%async_computation.12 | async-start | bytes 786432 | tf_op jit(solution)/shard_map/psum | solution.py:389
  1157.6 5.5 copy-start.83
  1157.6 5.5 copy-start.66
  1157.6 5.5 copy-start.6
  1157.6 5.8 copy-start.24
  1166.3 7.0 copy-start.91
  1166.3 422.2 %copy-start.46 = (f32[1,24,96,96]{3,2,1,0:T(8,128)S(1)}, f32[1,24,96,96]{3,2,1,0:T(8,128)}, u32[]{:S(2)}) copy-start(f32[1,24,96,96]{3,2,1,0:T(8,128)} %param.32) | copy-start | bytes 2654212
  1588.5 5.2 copy-start.43
  1588.5 5.2 copy-start.73
  1593.7 4.8 copy-start.18
  1593.7 4.7 copy-start.74
  1599.3 5.6 copy-start.28
  1601.3 4.4 copy-start.63
  1601.3 4.4 copy-start.64
  1601.3 4.4 copy-start.89
  1601.3 4.4 copy-start.90
  1604.9 3.9 copy-start.48
  1605.7 8.2 copy-start.49
  (68 other events, 137.4 us)
Sparse Core Ops, SparseCore 0:
  10.8 82.6 all-gather.15
  95.6 44.5 all-gather.13
  230.5 99.0 reduce-scatter.4
  339.6 46.3 all-gather.7
  451.1 99.0 reduce-scatter.6
  616.2 47.3 all-gather.9
  694.6 99.0 reduce-scatter.8
  805.8 46.3 all-gather.11
  1040.8 99.0 reduce-scatter.10
  1153.9 298.4 all-reduce.3
  1458.2 126.4 all-reduce.5
where the time goes:
time: 1640 us; the launch traced here: 1630 us
  waiting for transfers between devices  886 us (54%)
  matrix products  321 us (20%)
  other arithmetic  180 us (11%)
  local copies, waits for them, and re-layouts  136 us (8%)
  blocking collectives  79.6 us (5%)
  between operations  22.7 us (1%)
    psum x1, waiting for transfers between devices, body(): summed_all = lax.psum(slot_grads, 'dp')  278 us
    reduce_scatter x2, waiting for transfers between devices, merge_rows(): return lax.psum_scatter(values, 'tensor', scatter_dimension=0, tiled=True)  198 us
    reduce_scatter x2, waiting for transfers between devices, merge_grads(): return lax.psum_scatter(values, 'tensor', scatter_dimension=0, tiled=True)  99.2 us
    all_gather x2, waiting for transfers between devices, spread_grads(): return lax.all_gather(values, 'tensor', axis=0, tiled=True)  89.9 us
    psum x1, waiting for transfers between devices, body(): lax.psum((embedding_clipped_gradient, norm_grad), ('dp', 'tensor'))  84.2 us
    psum x2, blocking collectives, body(): lax.psum((-jnp.sum(mask_values * picked), jnp.sum(mask_values)), ('dp', '...  79.6 us
    all_gather x1, waiting for transfers between devices, body(): lax.all_gather(block_weight[0].astype(bf16), 'dp', axis=0, tiled=True)[None]  73.8 us
    all_gather x2, waiting for transfers between devices, spread_rows(): return lax.all_gather(values, 'tensor', axis=0, tiled=True)  62.8 us
  transfers between devices with their start and end apart: 11, of which 10 were waited for; matrix products, arithmetic and copies ran while one was open for 11% of the time, Pallas kernels for 0%

commit v1 on v0

v1 whole, which is shorter than its diff:
```python
import math

import jax
import jax.numpy as jnp
from jax import lax
from jax.sharding import PartitionSpec as P

FF = 3072
HS = 64


CLIP_LEVEL = 0.005
STAT_DECAY = 0.5
MATRIX_RATE = 0.03
WEIGHT_DECAY = 0.01
VECTOR_RATE = 0.2
FIRST_BETA = 0.9
SECOND_BETA = 0.999
ADAM_EPSILON = 1e-08
NORM_EPSILON = 1e-05
ROOT_EPSILON = 1e-06
MASK_VALUE = -1e30
ROTARY_BASE = 10000.0
TOP_PRECISION = lax.Precision.HIGHEST


def layer_norm(values, gain_row, bias_row):
    center = values - jnp.mean(values, -1, keepdims=True)
    spread = jnp.mean(center * center, -1, keepdims=True)
    return center * lax.rsqrt(spread + NORM_EPSILON) * gain_row + bias_row


def exact_gelu(values):
    return jax.nn.gelu(values, approximate=False)


def rotary_tables(length, width):
    half_width = width // 2
    freqs = jnp.exp(
        -math.log(ROTARY_BASE) * (2.0 * jnp.arange(half_width, dtype=jnp.float32) / width)
    )
    angles = jnp.arange(length, dtype=jnp.float32)[:, None] * freqs[None, :]
    return (jnp.cos(angles), jnp.sin(angles))


def rotate(values, cosine, sine):
    half_width = values.shape[-1] // 2
    front = values[..., :half_width]
    behind = values[..., half_width:]
    cos_col = cosine[:, None, :]
    sin_col = sine[:, None, :]
    return jnp.concatenate(
        [front * cos_col - behind * sin_col, behind * cos_col + front * sin_col], -1
    )


def block_parts(ordered, width, shard_width, shard_ff, edge):
    shards = ordered.shape[0]
    model = width // edge
    wide = shard_width // edge
    tall = shard_ff // edge
    ends = [3 * wide * model, wide * model, model * tall, tall * model]
    pieces = []
    offset = 0
    for count in ends:
        pieces.append(ordered[:, offset : offset + count])
        offset += count
    project = pieces[0].reshape(shards, model, 3, wide, edge, edge)
    project = project.transpose(1, 4, 2, 0, 3, 5).reshape(width, 3 * shards * shard_width)
    outward = pieces[1].reshape(shards, wide, model, edge, edge)
    outward = outward.transpose(0, 1, 3, 2, 4).reshape(shards * shard_width, width)
    expand = pieces[2].reshape(shards, model, tall, edge, edge)
    expand = expand.transpose(1, 3, 0, 2, 4).reshape(width, shards * shard_ff)
    contract = pieces[3].reshape(shards, tall, model, edge, edge)
    contract = contract.transpose(0, 1, 3, 2, 4).reshape(shards * shard_ff, width)
    return project, outward, expand, contract


def parts_to_blocks(parts, width, shards, shard_width, shard_ff, edge):
    model = width // edge
    wide = shard_width // edge
    tall = shard_ff // edge
    project, outward, expand, contract = parts
    project = project.reshape(model, edge, 3, shards, wide, edge).transpose(3, 0, 2, 4, 1, 5)
    outward = outward.reshape(shards, wide, edge, model, edge).transpose(0, 1, 3, 2, 4)
    expand = expand.reshape(model, edge, shards, tall, edge).transpose(2, 0, 3, 1, 4)
    contract = contract.reshape(shards, tall, edge, model, edge).transpose(0, 1, 3, 2, 4)
    return jnp.concatenate(
        [piece.reshape(shards, -1, edge, edge) for piece in (project, outward, expand, contract)], 1
    )


def masked_scores(chosen, keys, segment, offset, block_rows):
    same = segment[offset : offset + block_rows, None] == segment[None, :]
    scores = jnp.einsum("qhd,khd->hqk", chosen, keys, preferred_element_type=jnp.float32)
    return jnp.where(same[None], scores, MASK_VALUE)


def attend_forward(query, keys, values, segment):
    length = query.shape[0]
    block_rows = min(512, length)
    outputs = []
    totals = []
    for offset in range(0, length, block_rows):
        scores = masked_scores(
            query[offset : offset + block_rows], keys, segment, offset, block_rows
        )
        top_score = jnp.max(scores, -1, keepdims=True)
        weights = jnp.exp(scores - top_score)
        summed = jnp.sum(weights, -1, keepdims=True)
        probs = weights / summed
        outputs.append(
            jnp.einsum(
                "hqk,khd->qhd",
                probs.astype(jnp.bfloat16),
                values,
                preferred_element_type=jnp.float32,
            )
        )
        totals.append((top_score + jnp.log(summed))[..., 0])
    return (jnp.concatenate(outputs, 0), jnp.concatenate(totals, 1))


def attend_backward(query, keys, values, segment, grad_out, log_total):
    length = query.shape[0]
    block_rows = min(512, length)
    query_parts = []
    key_grad = jnp.zeros(keys.shape, jnp.float32)
    value_grad = jnp.zeros(values.shape, jnp.float32)
    for offset in range(0, length, block_rows):
        chosen = query[offset : offset + block_rows]
        grad_block = grad_out[offset : offset + block_rows]
        scores = masked_scores(chosen, keys, segment, offset, block_rows)
        probs = jnp.exp(scores - log_total[:, offset : offset + block_rows, None])
        grad_probs = jnp.einsum(
            "qhd,khd->hqk", grad_block, values, preferred_element_type=jnp.float32
        )
        delta = jnp.sum(probs * grad_probs, -1, keepdims=True)
        grad_scores = (probs * (grad_probs - delta)).astype(jnp.bfloat16)
        query_parts.append(
            jnp.einsum("hqk,khd->qhd", grad_scores, keys, preferred_element_type=jnp.float32)
        )
        key_grad = key_grad + jnp.einsum(
            "hqk,qhd->khd", grad_scores, chosen, preferred_element_type=jnp.float32
        )
        value_grad = value_grad + jnp.einsum(
            "hqk,qhd->khd",
            probs.astype(jnp.bfloat16),
            grad_block,
            preferred_element_type=jnp.float32,
        )
    return (jnp.concatenate(query_parts, 0), key_grad, value_grad)


def shampoo(grad, left, right, left_root, right_root, weight):
    new_left = STAT_DECAY * left + (1.0 - STAT_DECAY) * jnp.einsum(
        "...ij,...kj->...ik", grad, grad, precision=TOP_PRECISION
    )
    new_right = STAT_DECAY * right + (1.0 - STAT_DECAY) * jnp.einsum(
        "...ji,...jk->...ik", grad, grad, precision=TOP_PRECISION
    )
    partial_left = jnp.einsum("...ij,...jk->...ik", left_root, grad, precision=TOP_PRECISION)
    precond = jnp.einsum("...ij,...jk->...ik", partial_left, right_root, precision=TOP_PRECISION)
    scale_back = lax.rsqrt(jnp.mean(precond * precond, axis=(-2, -1), keepdims=True) + ROOT_EPSILON)
    new_weight = weight * (1.0 - MATRIX_RATE * WEIGHT_DECAY) - MATRIX_RATE * precond * scale_back
    return (new_left, new_right, new_weight)


def adamw(grad, moment, second, weight, step_value):
    new_moment = FIRST_BETA * moment + (1.0 - FIRST_BETA) * grad
    new_second = SECOND_BETA * second + (1.0 - SECOND_BETA) * grad * grad
    corrected_one = new_moment / (1.0 - FIRST_BETA**step_value)
    corrected_two = new_second / (1.0 - SECOND_BETA**step_value)
    new_weight = weight - VECTOR_RATE * (
        corrected_one / (jnp.sqrt(corrected_two) + ADAM_EPSILON) + WEIGHT_DECAY * weight
    )
    return (new_moment, new_second, new_weight)


def body(
    codons,
    segments,
    targets,
    loss_mask,
    owner_map,
    step_count,
    block_weight,
    block_left,
    block_right,
    block_left_root,
    block_right_root,
    embedding_weight,
    table_left,
    table_right,
    table_left_root,
    table_right_root,
    norm_params,
    norm_moment,
    norm_second,
):
    width = embedding_weight.shape[1]
    vocab_size = embedding_weight.shape[0]
    shards = lax.axis_size("tensor")
    owners = lax.axis_size("dp")
    shard_width = width // shards
    shard_ff = FF // shards
    block_edge = block_weight.shape[-1]
    slot_count = block_weight.shape[1]
    block_total = owner_map.shape[0]
    heads = width // HS
    length = codons.shape[1]
    bf16 = jnp.bfloat16
    single_float = jnp.float32

    gathered = lax.all_gather(block_weight[0].astype(bf16), ("dp", "tensor"), axis=0, tiled=False)
    gathered = gathered.reshape(owners, shards, slot_count, block_edge, block_edge)
    by_shard = gathered.transpose(1, 0, 2, 3, 4).reshape(shards, block_total, block_edge, block_edge)
    ordered = by_shard[:, owner_map]
    parts = block_parts(ordered, width, shard_width, shard_ff, block_edge)
    project, outward, expand, contract = parts

    vocab_index = jnp.arange(vocab_size, dtype=jnp.int32)
    codon_hot = (codons[0][:, None] == vocab_index).astype(single_float)
    embed_scale = math.sqrt(width)
    embedded = embed_scale * jnp.dot(codon_hot, embedding_weight, precision=TOP_PRECISION)
    normed = layer_norm(embedded, norm_params[0], norm_params[1]).astype(bf16)
    projected = jnp.dot(normed, project, preferred_element_type=single_float)
    cosine, sine = rotary_tables(length, HS)

    def heads_of(component):
        return projected[:, component * width : (component + 1) * width].reshape(length, heads, HS)

    query = (rotate(heads_of(0), cosine, sine) * HS ** (-0.5)).astype(bf16)
    keys = rotate(heads_of(1), cosine, sine).astype(bf16)
    values = heads_of(2).astype(bf16)
    row_index = lax.axis_index("tensor")
    segment = lax.dynamic_index_in_dim(segments, row_index, 0, keepdims=False)
    attended, log_total = attend_forward(query, keys, values, segment)
    attended = attended.astype(bf16).reshape(length, width)
    middle = embedded + jnp.dot(attended, outward, preferred_element_type=single_float)
    normed_two = layer_norm(middle, norm_params[2], norm_params[3]).astype(bf16)
    hidden = jnp.dot(normed_two, expand, preferred_element_type=single_float)
    active = exact_gelu(hidden).astype(bf16)
    final_in = middle + jnp.dot(active, contract, preferred_element_type=single_float)
    final = layer_norm(final_in, norm_params[4], norm_params[5])
    final_low = final.astype(bf16)
    table_low = embedding_weight.astype(bf16)
    scores = jnp.einsum("xt,qt->xq", final_low, table_low, preferred_element_type=single_float)
    shifted = scores - jnp.max(scores, -1, keepdims=True)
    log_probs = shifted - jnp.log(jnp.sum(jnp.exp(shifted), -1, keepdims=True))
    target_hot = (targets[0][:, None] == vocab_index).astype(single_float)
    mask_values = loss_mask[0].astype(single_float)
    picked = jnp.sum(target_hot * log_probs, -1)
    loss_sum, mask_total = lax.psum(
        (-jnp.sum(mask_values * picked), jnp.sum(mask_values)), ("dp", "tensor")
    )
    token_count = jnp.maximum(mask_total, 1.0)
    loss_value = loss_sum / token_count
    logit_grad = (
        (jnp.exp(log_probs) - target_hot) * (mask_values / token_count)[:, None]
    ).astype(bf16)
    table_grad = jnp.einsum("ux,up->xp", logit_grad, final_low, preferred_element_type=single_float)
    final_grad = jnp.dot(logit_grad, table_low, preferred_element_type=single_float)
    _, final_back = jax.vjp(layer_norm, final_in, norm_params[4], norm_params[5])
    grad_final_in, gain_five, bias_five = final_back(final_grad)
    d_two = grad_final_in.astype(bf16)
    contract_grad = jnp.einsum("lk,le->ke", active, d_two, preferred_element_type=single_float)
    grad_active = jnp.einsum("le,ke->lk", d_two, contract, preferred_element_type=single_float)
    _, gelu_back = jax.vjp(exact_gelu, hidden)
    hidden_grad = gelu_back(grad_active)[0].astype(bf16)
    expand_grad = jnp.einsum("lz,lx->zx", normed_two, hidden_grad, preferred_element_type=single_float)
    grad_normed_two = jnp.einsum(
        "lx,zx->lz", hidden_grad, expand, preferred_element_type=single_float
    )
    _, second_back = jax.vjp(layer_norm, middle, norm_params[2], norm_params[3])
    grad_middle_norm, gain_three, bias_three = second_back(grad_normed_two)
    grad_middle = grad_final_in + grad_middle_norm
    d_one = grad_middle.astype(bf16)
    outward_grad = jnp.einsum("lk,lx->kx", attended, d_one, preferred_element_type=single_float)
    grad_attended = jnp.einsum("lc,vc->lv", d_one, outward, preferred_element_type=single_float)
    grad_attended = grad_attended.astype(bf16).reshape(length, heads, HS)
    grad_query, grad_keys, grad_values = attend_backward(
        query, keys, values, segment, grad_attended, log_total
    )
    grad_projected = jnp.concatenate(
        [
            rotate(grad_query * HS ** (-0.5), cosine, -sine).reshape(length, width),
            rotate(grad_keys, cosine, -sine).reshape(length, width),
            grad_values.reshape(length, width),
        ],
        -1,
    ).astype(bf16)
    project_grad = jnp.einsum(
        "lh,lf->hf", normed, grad_projected, preferred_element_type=single_float
    )
    grad_normed = jnp.einsum(
        "lf,hf->lh", grad_projected, project, preferred_element_type=single_float
    )
    _, first_back = jax.vjp(layer_norm, embedded, norm_params[0], norm_params[1])
    grad_embed_norm, gain_one, bias_one = first_back(grad_normed)
    embedded_grad = grad_middle + grad_embed_norm
    table_grad = table_grad + embed_scale * jnp.einsum(
        "ux,up->xp", codon_hot, embedded_grad, precision=TOP_PRECISION
    )
    norm_grad = jnp.stack([gain_one, bias_one, gain_three, bias_three, gain_five, bias_five])
    table_grad, norm_grad = lax.psum((table_grad, norm_grad), ("dp", "tensor"))
    block_grads = parts_to_blocks(
        (project_grad, outward_grad, expand_grad, contract_grad),
        width, shards, shard_width, shard_ff, block_edge,
    )
    slot_order = (
        jnp.zeros((block_total,), jnp.int32)
        .at[owner_map]
        .set(jnp.arange(block_total, dtype=jnp.int32))
    )
    slot_grads = block_grads[:, slot_order].reshape(
        shards, owners, slot_count, block_edge, block_edge
    )
    slot_grads = slot_grads.transpose(1, 0, 2, 3, 4).reshape(
        owners * shards * slot_count, block_edge, block_edge
    )
    owned = lax.psum_scatter(slot_grads, ("dp", "tensor"), scatter_dimension=0, tiled=True)
    embedding_clipped_gradient = table_grad
    square_sum = lax.psum(jnp.sum(owned * owned), ("dp", "tensor"))
    square_sum = (
        square_sum
        + jnp.sum(embedding_clipped_gradient * embedding_clipped_gradient)
        + jnp.sum(norm_grad * norm_grad)
    )
    grad_norm = jnp.sqrt(square_sum)
    factor = CLIP_LEVEL / jnp.maximum(grad_norm, CLIP_LEVEL)
    block_grad = owned * factor
    new_left, new_right, new_weight = shampoo(
        block_grad,
        block_left[0],
        block_right[0],
        block_left_root[0],
        block_right_root[0],
        block_weight[0],
    )
    table_clipped = embedding_clipped_gradient * factor
    table_left_new, table_right_new, table_weight_new = shampoo(
        table_clipped, table_left, table_right, table_left_root, table_right_root, embedding_weight
    )
    norm_clipped = norm_grad * factor
    moment_new, second_new, params_new = adamw(
        norm_clipped, norm_moment, norm_second, norm_params, step_count.astype(single_float)
    )
    return (
        loss_value,
        grad_norm,
        block_grad[None],
        new_left[None],
        new_right[None],
        new_weight[None],
        table_clipped,
        table_left_new,
        table_right_new,
        table_weight_new,
        norm_clipped,
        moment_new,
        second_new,
        params_new,
    )


def solution(mesh):
    in_specs = (
        P(("dp", "tensor"), None),
        P("dp", None),
        P(("dp", "tensor"), None),
        P(("dp", "tensor"), None),
        P(),
        P(),
        P("tensor", "dp", None, None),
        P("tensor", "dp", None, None),
        P("tensor", "dp", None, None),
        P("tensor", "dp", None, None),
        P("tensor", "dp", None, None),
        P(),
        P(),
        P(),
        P(),
        P(),
        P(),
        P(),
        P(),
    )
    out_specs = (
        P(),
        P(),
        P("tensor", "dp", None, None),
        P("tensor", "dp", None, None),
        P("tensor", "dp", None, None),
        P("tensor", "dp", None, None),
        P(),
        P(),
        P(),
        P(),
        P(),
        P(),
        P(),
        P(),
    )
    return jax.shard_map(body, mesh=mesh, in_specs=in_specs, out_specs=out_specs, check_vma=False)
```

time: 1640 us -> 1350 us (0.82)
  waiting for transfers between devices: 886 us -> 520 us
  local copies, waits for them, and re-layouts: 136 us -> 289 us
  other arithmetic: 180 us -> 135 us
  matrix products: 321 us -> 296 us
    psum x2 -> x1, waiting for transfers between devices: 362 us -> 131 us  [body(): table_grad, norm_grad = lax.psum((table_grad, norm_grad), ('dp', 'tensor'))]
    all_gather x5 -> x1, waiting for transfers between devices: 227 us -> 71.7 us  [body(): lax.all_gather(block_weight[0].astype(bf16), ('dp', 'tensor'), axis=0, ti...]
    reshape x8 -> x20, local copies, waits for them, and re-layouts: 22.5 us -> 142 us  [the longest x2 29.5 us: parts_to_blocks(): expand.reshape(model, edge, shards, tall, edge).transpose(2, 0, 3, 1, 4)]
    transpose x0 -> x2, local copies, waits for them, and re-layouts: none -> 47.6 us  [the longest x1 28.5 us: body(): slot_grads.transpose(1, 0, 2, 3, 4)]
    gather x2, local copies, waits for them, and re-layouts: 14.2 us -> 44.3 us  [the longest x1 27.6 us: body(): block_grads[:, slot_order]]
    convert_element_type x5 -> x4, other arithmetic: 36.4 us -> 6.92 us  [the longest x1 4.7 us: body(): d_one = grad_middle.astype(bf16)]
    another operation x6 -> x2, other arithmetic: 30.8 us -> 4.8 us  [the longest x1 28.1 us: exact_gelu(): return jax.nn.gelu(values, approximate=False)]
    all_gather x3 -> x0, local copies, waits for them, and re-layouts: 25.9 us -> none  [the longest x2 17.3 us: spread_grads(): return lax.all_gather(values, 'tensor', axis=0, tiled=True)]
  transfers between devices with their start and end apart: 11 -> 3, of which waited for: 10 -> 3; matrix products, arithmetic and copies ran while one was open for 11% -> 3% of each run, Pallas kernels for 0% -> 0%
where the time goes in v1:
time: 1350 us
  waiting for transfers between devices  520 us (39%)
  matrix products  296 us (22%)
  local copies, waits for them, and re-layouts  289 us (21%)
  other arithmetic  135 us (10%)
  blocking collectives  82.8 us (6%)
  between operations  23.1 us (2%)
    reduce_scatter x1, waiting for transfers between devices, body(): lax.psum_scatter(slot_grads, ('dp', 'tensor'), scatter_dimension=0, tiled...  317 us
    psum x1, waiting for transfers between devices, body(): table_grad, norm_grad = lax.psum((table_grad, norm_grad), ('dp', 'tensor'))  131 us
    psum x2, blocking collectives, body(): lax.psum((-jnp.sum(mask_values * picked), jnp.sum(mask_values)), ('dp', '...  82.8 us
    all_gather x1, waiting for transfers between devices, body(): lax.all_gather(block_weight[0].astype(bf16), ('dp', 'tensor'), axis=0, ti...  71.7 us
    convert_element_type x1, other arithmetic, attend_backward(): grad_scores = (probs * (grad_probs - delta)).astype(jnp.bfloat16)  41.5 us
    dot_general x1, matrix products, body(): hidden = jnp.dot(normed_two, expand, preferred_element_type=single_float)  37.4 us
    dot_general x2, matrix products, attend_backward(): jnp.einsum('qhd,khd->hqk', grad_block, values, preferred_element_type=jnp...  35.5 us
    reshape x2, local copies, waits for them, and re-layouts, parts_to_blocks(): expand.reshape(model, edge, shards, tall, edge).transpose(2, 0, 3, 1, 4)  29.5 us
  transfers between devices with their start and end apart: 3, of which 3 were waited for; matrix products, arithmetic and copies ran while one was open for 3% of the time, Pallas kernels for 0%

profile of v1, /device:TPU:0, one launch (start us, length us, event | category | flops | bytes accessed | tf_op | source)
XLA Modules:
  0.0 1346.4 jit_solution(12812759535601039246)
XLA Ops:
  10.9 43.0 %psum.36 = f32[]{:T(128)} all-reduce(f32[]{:T(128)} %convert_reduce_fusion), channel_id=1, replica_groups=mesh['dp'=8,'tensor'=4] {'dp','tensor'}, use_global_device_ids=true, to_apply=%region_16.17 | all-reduce | flops 1 | bytes 8 | tf_op jit(solution)/shard_map/psum | solution.py:254
  68.4 71.7 %all-gather.2.cloned.1.call-done = bf16[32,24,96,96]{3,2,1,0:T(8,128)(2,1)} async-done(((bf16[1,24,96,96]{3,2,1,0:T(8,128)(2,1)}), bf16[32,24,96,96]{3,2,1,0:T(8,128)(2,1)}) %all-gather.2.cloned.1.call-update) | async-done | bytes 14155792 | tf_op jit(solution)/shard_map/all_gather | solution.py:215
  140.0 19.0 %copy.76 = bf16[4,8,24,96,96]{4,3,2,1,0:T(8,128)(2,1)} copy(bf16[4,8,24,96,96]{4,3,2,0,1:T(8,128)(2,1)} %bitcast.174) | data formatting | bytes 28311552 | tf_op jit(solution)/shard_map/transpose | solution.py:217
  159.1 16.7 %gather_fusion = bf16[192,4,96,96]{3,2,1,0:T(8,128)(2,1)} fusion(bf16[4,192,96,96]{3,2,1,0:T(8,128)(2,1)} %bitcast.164, s32[1024]{0:T(1024)S(1)} %pad_clamp_fusion.1), kind=kCustom, calls=%fused_computation | custom fusion | bytes 28312320 | tf_op jit(solution)/shard_map/gather | solution.py:218
  175.8 5.9 slice.130
  181.7 7.0 copy.77
  188.7 8.2 reshape.396
  197.0 7.5 fusion.96
  204.5 3.5 fusion.102
  210.6 6.0 fusion.101
  216.7 3.5 copy.79
  220.2 3.6 copy.80
  226.5 3.8 subtract_convert_fusion.2
  230.8 10.5 select_reduce_fusion.1
  241.3 11.6 fusion
  253.5 12.4 fusion.41
  265.8 10.4 select_reduce_fusion
  276.2 11.5 fusion.1
  287.7 12.7 fusion.40
  303.2 2.9 reshape.400
  306.2 4.4 fusion.104
  312.7 6.9 copy.104
  319.6 12.5 reshape.402
  332.1 12.6 copy.103
  344.7 10.8 reshape.404
  355.6 37.4 %multiply_convert_fusion.2 = (bf16[1024,3072]{1,0:T(8,128)(2,1)S(1)}, f32[1024,3072]{1,0:T(8,128)}, f32[1024,3072]{1,0:T(8,128)}) fusion(bf16[768,3072]{1,0:T(8,128)(2,1)} %reshape.402, f32[1024,768]{0,1:T(8,128)} %copy-done.8, f32[768]{0:T(1024)S(1)} %copy-done.107, f32[768]{0:T(1024)S(1)} %copy-done.80, f32[1024]{0:T(1024)S(1)} %fusion.82, ...), kind=kOutput, calls=%fused_computation.27 | convolution fusion | flops 5040242688 | bytes 39335936 | tf_op jit(solution)/shard_map/dot_general | solution.py:242
  393.0 5.3 fusion.105
  406.0 18.9 %add_convert_fusion = bf16[1024,3072]{1,0:T(8,128)(2,1)} fusion(f32[1024,3072]{1,0:T(8,128)} %get-tuple-element.40, f32[1024,3072]{1,0:T(8,128)} %get-tuple-element.76, bf16[3072,768]{1,0:T(8,128)(2,1)} %reshape.404, f32[1024,768]{0,1:T(8,128)} %get-tuple-element.38, f32[1024]{0:T(1024)S(1)} %negate_multiply_fusion.3), kind=kOutput, calls=%fused_computation.25 | convolution fusion | flops 4877451264 | bytes 39325696 | tf_op jit(solution)/shard_map/le,ke->lk/dot_general | solution.py:268
  424.9 10.5 multiply_reduce_fusion.3
  442.6 18.0 %multiply_reduce_fusion.1 = (f32[12,512]{1,0:T(8,128)S(1)}, f32[12,512,1024]{2,1,0:T(8,128)}) fusion(f32[12,512,1024]{2,1,0:T(8,128)} %get-tuple-element.73, f32[12,512]{1,0:T(8,128)S(1)} %copy-done.56, pred[512,1024]{1,0:T(8,128)(4,1)S(1)} %copy-done.19, bf16[512,12,64]{0,2,1:T(8,128)(2,1)} %bitcast.183, bf16[1024,12,64]{0,2,1:T(8,128)(2,1)} %bitcast.177), kind=kOutput, calls=%fused_computation.8 | convolution fusion | flops 830466048 | bytes 53264384 | tf_op jit(solution)/shard_map/qhd,khd->hqk/dot_general | solution.py:135
  460.6 17.5 %multiply_reduce_fusion = (f32[12,512]{1,0:T(8,128)S(1)}, f32[12,512,1024]{2,1,0:T(8,128)}) fusion(f32[12,512,1024]{2,1,0:T(8,128)} %get-tuple-element.71, f32[12,512]{1,0:T(8,128)S(1)} %copy-done.58, pred[512,1024]{1,0:T(8,128)(4,1)S(1)} %copy-done.21, bf16[512,12,64]{0,2,1:T(8,128)(2,1)} %bitcast.185, bf16[1024,12,64]{0,2,1:T(8,128)(2,1)} %bitcast.178), kind=kOutput, calls=%fused_computation.5 | convolution fusion | flops 830466048 | bytes 53264384 | tf_op jit(solution)/shard_map/qhd,khd->hqk/dot_general | solution.py:135
  478.2 41.5 %multiply_convert_fusion = (bf16[12,512,1024]{2,1,0:T(8,128)(2,1)}, bf16[12,512,1024]{2,1,0:T(8,128)(2,1)}) fusion(f32[12,512,1024]{2,1,0:T(8,128)} %get-tuple-element.84, f32[12,512,1024]{2,1,0:T(8,128)} %get-tuple-element.71, f32[12,512]{1,0:T(8,128)S(1)} %get-tuple-element.83, f32[12,512]{1,0:T(8,128)S(1)} %copy-done.58, ...), kind=kLoop, calls=%fused_computation.4 | loop fusion | flops 62914560 | bytes 126976000 | tf_op jit(solution)/shard_map/convert_element_type | solution.py:139
  519.7 7.2 fusion.60
  526.9 9.7 convolution_bitcast_fusion.1
  536.7 13.1 fusion.4
  549.9 4.7 fusion.24
  556.0 10.6 fusion.94
  566.7 7.9 fusion.64
  574.6 9.7 convolution_bitcast_fusion
  584.3 7.3 add_bitcast_fusion
  591.7 12.8 add_convert_fusion.1
  609.9 7.0 fusion.31
  616.9 14.9 %reshape.408 = f32[8,96,3,4,2,96]{5,4,3,2,1,0:T(2,128)} reshape(f32[768,2304]{1,0:T(8,128)} %fusion.31) | data formatting | bytes 14155776 | tf_op jit(solution)/shard_map/reshape | solution.py:84
  631.8 9.1 copy.84
  640.9 13.2 reshape.411
  654.0 16.3 %copy.85 = f32[8,96,4,8,96]{4,1,3,0,2:T(8,128)} copy(f32[8,96,4,8,96]{4,3,2,1,0:T(8,128)} %reshape.411) | data formatting | bytes 18874368 | tf_op jit(solution)/shard_map/reshape | solution.py:86
  670.4 13.9 %reshape.413 = f32[4,8,96,8,96]{4,3,2,1,0:T(8,128)} reshape(f32[3072,768]{1,0:T(8,128)} %fusion.64) | data formatting | bytes 18874368 | tf_op jit(solution)/shard_map/reshape | solution.py:87
  684.3 11.4 copy.86
  695.7 3.5 fusion.108
  699.2 25.5 %pad_maximum_fusion = f32[4,192,96,96]{3,2,1,0:T(8,128)} fusion(f32[4,64,96,96]{3,2,1,0:T(8,128)} %bitcast.166, f32[4,64,96,96]{3,2,1,0:T(8,128)} %bitcast.165, f32[4,16,96,96]{3,2,1,0:T(8,128)} %bitcast.189, f32[4,48,96,96]{3,2,1,0:T(8,128)} %bitcast.167), kind=kLoop, calls=%fused_computation.3 | loop fusion | flops 21233664 | bytes 56623104 | tf_op jit(solution)/shard_map/concatenate | solution.py:88
  724.7 27.6 %gather_fusion.1 = f32[192,4,96,96]{3,2,1,0:T(8,128)} fusion(f32[4,192,96,96]{3,2,1,0:T(8,128)} %pad_maximum_fusion, s32[1024]{0:T(1024)} %pad_clamp_fusion), kind=kCustom, calls=%fused_computation.1 | custom fusion | bytes 56623872 | tf_op jit(solution)/shard_map/gather | solution.py:316
  752.4 28.5 %copy.88 = f32[8,4,24,96,96]{4,3,2,1,0:T(8,128)} copy(f32[8,4,24,96,96]{4,3,1,2,0:T(8,128)} %bitcast.157) | data formatting | bytes 56623104 | tf_op jit(solution)/shard_map/transpose | solution.py:319
  781.0 9.0 fusion.107
  790.0 4.5 copy.89
  794.5 4.5 multiply_reduce_fusion.5
  805.9 3.8 fusion.45
  811.3 316.8 %reduce-scatter.2.cloned.1.call-done = f32[24,96,96]{2,1,0:T(8,128)} async-done(((f32[768,96,96]{2,1,0:T(8,128)}), f32[24,96,96]{2,1,0:T(8,128)}) %reduce-scatter.2.cloned.1.call-update) | async-done | bytes 884752 | tf_op jit(solution)/shard_map/reduce_scatter | solution.py:322
  1130.3 131.2 %all-reduce.3.cloned.1.call-done = f32[128,768]{1,0:T(8,128)} async-done(((f32[128,768]{1,0:T(8,128)}), f32[128,768]{1,0:T(8,128)}) %all-reduce.3.cloned.1.call-update) | async-done | bytes 393232 | tf_op jit(solution)/shard_map/psum | solution.py:306
  1263.1 39.8 %all-reduce = (f32[]{:T(128)}, f32[]{:T(128)}, f32[6,768]{1,0:T(8,128)S(1)}) all-reduce(f32[]{:T(128)S(6)} %neg.35, f32[]{:T(128)} %multiply_reduce_fusion.13, f32[6,768]{1,0:T(8,128)S(1)} %stack.2), channel_id=1, replica_groups=mesh['dp'=8,'tensor'=4] {'dp','tensor'}, use_global_device_ids=true, to_apply=%region_14.15 | all-reduce | flops 4610 | bytes 36880 | tf_op jit(solution)/shard_map/psum | solution.py:254
  1308.2 2.8 multiply_reduce_fusion.14
  1311.7 5.5 add_multiply_fusion
  1326.0 2.9 fusion.52
  1330.7 3.1 fusion.39
  1333.8 3.6 fusion.38
  (322 shorter events, 73.8 us)
Async XLA Ops:
  7.2 1301.0 %copy-start = (f32[768,768]{1,0:T(8,128)S(1)}, f32[768,768]{1,0:T(8,128)}, u32[]{:S(2)}) copy-start(f32[768,768]{1,0:T(8,128)} %param.34) | copy-start | bytes 7077892
  7.2 132.9 %all-gather.2.cloned.1.call-start = ((), (), s32[]{:S(2)}) async-start(), calls=%async_computation.1 | async-start | bytes 19464192 | tf_op jit(solution)/shard_map/all_gather | solution.py:215
  9.6 1118.5 %reduce-scatter.2.cloned.1.call-start = ((), (), s32[]{:S(2)}) async-start(), calls=%async_computation.2 | async-start | bytes 38928384 | tf_op jit(solution)/shard_map/reduce_scatter | solution.py:322
  61.5 135.5 %copy-start.86 = (f32[768]{0:T(1024)}, f32[768]{0:T(1024)S(1)}, u32[]{:S(2)}) copy-start(f32[768]{0:T(1024)S(1)} %get-tuple-element.26) | copy-start | bytes 9220
  64.2 132.8 %copy-start.68 = (f32[1024]{0:T(1024)}, f32[1024]{0:T(1024)S(1)}, u32[]{:S(2)}) copy-start(f32[1024]{0:T(1024)S(1)} %broadcast_multiply_fusion.4) | copy-start | bytes 12292
  66.4 130.6 %copy-start.92 = (f32[1024]{0:T(1024)}, f32[1024]{0:T(1024)S(1)}, u32[]{:S(2)}) copy-start(f32[1024]{0:T(1024)S(1)} %fusion.81) | copy-start | bytes 12292
  67.7 158.8 %copy-start.46 = (f32[1024,32]{0,1:T(8,128)}, f32[1024,32]{0,1:T(8,128)S(1)}, u32[]{:S(2)}) copy-start(f32[1024,32]{0,1:T(8,128)S(1)} %get-tuple-element.67) | copy-start | bytes 393220
  68.4 185.1 %copy-start.18 = (pred[512,1024]{1,0:T(8,128)(4,1)}, pred[512,1024]{1,0:T(8,128)(4,1)S(1)}, u32[]{:S(2)}) copy-start(pred[512,1024]{1,0:T(8,128)(4,1)S(1)} %get-tuple-element.63) | copy-start | bytes 1572868
  68.4 219.4 %copy-start.20 = (pred[512,1024]{1,0:T(8,128)(4,1)}, pred[512,1024]{1,0:T(8,128)(4,1)S(1)}, u32[]{:S(2)}) copy-start(pred[512,1024]{1,0:T(8,128)(4,1)S(1)} %get-tuple-element.64) | copy-start | bytes 1572868
  188.7 8.2 copy-start.105
  197.0 12.4 slice-start
  197.0 12.4 slice-start.1
  197.0 12.3 slice-start.2
  197.0 12.3 slice-start.3
  230.3 35.5 %copy-start.14 = (bf16[1024,12,32]{0,2,1:T(8,128)(2,1)}, bf16[1024,12,32]{0,2,1:T(8,128)(2,1)S(1)}, u32[]{:S(2)}) copy-start(bf16[1024,12,32]{0,2,1:T(8,128)(2,1)S(1)} %get-tuple-element.49) | copy-start | bytes 2359300
  230.3 35.5 %copy-start.16 = (bf16[1024,12,32]{0,2,1:T(8,128)(2,1)}, bf16[1024,12,32]{0,2,1:T(8,128)(2,1)S(1)}, u32[]{:S(2)}) copy-start(bf16[1024,12,32]{0,2,1:T(8,128)(2,1)S(1)} %get-tuple-element.50) | copy-start | bytes 2359300
  230.8 35.1 %copy-start.22 = (bf16[1024,12,64]{0,2,1:T(8,128)(2,1)}, bf16[1024,12,64]{0,2,1:T(8,128)(2,1)S(1)}, u32[]{:S(2)}) copy-start(bf16[1024,12,64]{0,2,1:T(8,128)(2,1)S(1)} %fusion.26) | copy-start | bytes 4718596
  241.3 12.2 copy-start.23
  287.7 13.3 copy-start.31
  306.2 6.5 slice-start.5
  306.2 6.5 slice-start.6
  312.7 6.9 copy-start.84
  312.7 122.7 %copy-start.78 = (f32[1024]{0:T(1024)}, f32[1024]{0:T(1024)S(1)}, u32[]{:S(2)}) copy-start(f32[1024]{0:T(1024)S(1)} %fusion.82) | copy-start | bytes 12292
  344.7 10.9 copy-start.80
  344.7 10.9 copy-start.107
  355.6 37.4 %copy-start.9 = (f32[1024,768]{0,1:T(8,128)S(1)}, f32[1024,768]{0,1:T(8,128)}, u32[]{:S(2)}) copy-start(f32[1024,768]{0,1:T(8,128)} %copy-done.8) | copy-start | bytes 9437188
  355.6 37.4 %copy-start.35 = (bf16[3072,768]{1,0:T(8,128)(2,1)S(1)}, bf16[3072,768]{1,0:T(8,128)(2,1)}, u32[]{:S(2)}) copy-start(bf16[3072,768]{1,0:T(8,128)(2,1)} %reshape.404) | copy-start | bytes 14155780
  393.0 5.3 copy-start.109
  406.0 31.2 %copy-start.94 = (f32[1024]{0:T(1024)}, f32[1024]{0:T(1024)S(1)}, u32[]{:S(2)}) copy-start(f32[1024]{0:T(1024)S(1)} %negate_multiply_fusion.3) | copy-start | bytes 12292
  424.9 10.5 copy-start.85
  424.9 10.6 copy-start.10
  442.6 18.0 %copy-start.21 = (pred[512,1024]{1,0:T(8,128)(4,1)S(1)}, pred[512,1024]{1,0:T(8,128)(4,1)}, u32[]{:S(2)}) copy-start(pred[512,1024]{1,0:T(8,128)(4,1)} %copy-done.20) | copy-start | bytes 1572868
  442.6 18.0 %copy-start.58 = (f32[12,512]{1,0:T(8,128)S(1)}, f32[12,512]{1,0:T(8,128)}, u32[]{:S(2)}) copy-start(f32[12,512]{1,0:T(8,128)} %log_add_fusion) | copy-start | bytes 73732
  519.7 7.2 copy-start.15
  519.7 7.2 copy-start.17
  536.7 13.1 copy-start.2
  536.7 13.1 copy-start.11
  536.7 13.1 copy-start.13
  536.7 13.1 copy-start.73
  536.7 13.1 copy-start.75
  536.7 13.1 copy-start.79
  536.7 13.1 copy-start.81
  536.7 13.1 copy-start.95
  536.7 13.1 copy-start.98
  549.9 6.1 copy-start.108
  549.9 16.8 %slice-start.7 = ((s8[6291456]{0:T(1024)(128)(4,1)}), s8[4194304]{0:T(1024)(128)(4,1)S(1)}, s32[]{:S(2)}) async-start(s8[6291456]{0:T(1024)(128)(4,1)} %bitcast.211), calls=%async_computation.11 | async-start | bytes 8388608
  556.0 10.7 copy-start.37
  556.0 10.7 slice-start.8
  584.3 7.3 copy-start.30
  591.7 12.9 copy-start.33
  591.7 12.9 copy-start.34
  684.3 11.5 copy-start.42
  684.3 11.4 copy-start.43
  780.9 480.5 %all-reduce.3.cloned.1.call-start = ((), (), s32[]{:S(2)}) async-start(), calls=%async_computation.3 | async-start | bytes 786432 | tf_op jit(solution)/shard_map/psum | solution.py:306
  790.0 9.0 copy-start.83
  794.5 6.6 copy-start.7
  794.5 7.9 copy-start.60
  794.5 7.9 copy-start.66
  794.5 7.9 copy-start.71
  794.5 7.9 copy-start.77
  805.9 501.5 %copy-start.67 = (f32[128,128]{1,0:T(8,128)S(1)}, f32[128,128]{1,0:T(8,128)}, u32[]{:S(2)}) copy-start(f32[128,128]{1,0:T(8,128)} %param.33) | copy-start | bytes 196612
  1303.0 8.7 copy-start.62
  1311.7 7.9 copy-start.6
  1311.7 7.9 copy-start.48
  (58 other events, 181.9 us)
Sparse Core Ops, SparseCore 0:
  11.5 128.4 all-gather.1
  781.0 346.9 reduce-scatter.1
  1134.8 126.5 all-reduce.2
